TPU v7x, 32 devices: a whole 2x2x4 slice. The times are simulated.
32 devices in a mesh: fsdp: 4 (over x, core), ctx: 4 (over z), tp: 2 (over y).
Axes of the slice: x: 2, y: 2, z: 4, core: 2. Of those that a mesh axis runs over, the one named last changes fastest.
Arguments:
- tokens: bfloat16 [8, 4096, 768], P('fsdp', 'ctx'), may hold values from -6 to 6
- qkv_weight: bfloat16 [768, 3, 768], P(('fsdp', 'ctx'), None, 'tp'), may hold values from -0.21875 to 0.21875
- qv_bias: bfloat16 [2, 768], P(None, 'tp'), may hold values from -3 to 3
- out_weight: bfloat16 [768, 768], P(('fsdp', 'ctx'), 'tp'), may hold values from -8 to 8
- up_weight: bfloat16 [768, 3072], P(('fsdp', 'ctx'), 'tp'), may hold values from -0.21875 to 0.21875
- up_bias: bfloat16 [3072], P('tp'), may hold values from -3 to 3
- down_weight: bfloat16 [768, 3072], P(('fsdp', 'ctx'), 'tp'), may hold values from -0.109375 to 0.109375
- norm_gains: bfloat16 [768, 2], P(('fsdp', 'ctx')), may hold values from 0.5 to 1.5
- row_biases: bfloat16 [768, 4], P(('fsdp', 'ctx')), may hold values from -3 to 3
- cotangent: bfloat16 [8, 4096, 768], P('fsdp', 'ctx'), may hold values from -6 to 6
Outputs:
- output: bfloat16 [8, 4096, 768], P('fsdp', ('ctx', 'tp'))
- tokens_grad: bfloat16 [8, 4096, 768], P('fsdp', ('ctx', 'tp'))
- qkv_weight_grad: float32 [768, 3, 768], P(('fsdp', 'ctx'), None, 'tp')
- qv_bias_grad: float32 [2, 768], P(None, 'tp')
- out_weight_grad: float32 [768, 768], P(('fsdp', 'ctx'), 'tp')
- up_weight_grad: float32 [768, 3072], P(('fsdp', 'ctx'), 'tp')
- up_bias_grad: float32 [3072], P('tp')
- down_weight_grad: float32 [768, 3072], P(('fsdp', 'ctx'), 'tp')
- norm_gains_grad: float32 [768, 2], P(('fsdp', 'ctx'))
- row_biases_grad: float32 [768, 4], P(('fsdp', 'ctx'))
All inputs are finite; a program needn't handle non-finite values.
Results may differ from a plain program's by a relative error of at most 0.02.
Values may be sent and summed in bfloat16 or wider, within the bound.
No kernel may reach another device: no remote copies, remote signals or barrier semaphores. Data moves between devices by JAX's collectives and lax.ppermute only.
A program may use at most 256 MiB of HBM per device.

v0:
```python
import jax
import jax.numpy as jnp
from jax import lax
from jax.sharding import PartitionSpec as P

HD = 64
epsilon = 1e-12
score_scale = 0.125
highest = lax.Precision.HIGHEST


def contract_last(left, right):
    return lax.dot_general(
        left, right, (((1,), (1,)), ((), ())), preferred_element_type=jnp.float32
    )


def contract_first(left, right):
    return lax.dot_general(
        left, right, (((0,), (0,)), ((), ())), preferred_element_type=jnp.float32
    )


def norm_forward(hidden, gain, shift):
    center = hidden - jnp.mean(hidden, axis=-1, keepdims=True)
    inv_scale = lax.rsqrt(jnp.mean(center * center, axis=-1, keepdims=True) + epsilon)
    normed = center * inv_scale
    return (normed * gain + shift, normed, inv_scale)


def norm_backward(grad_out, normed, inv_scale, gain):
    grad_norm = grad_out * gain
    return inv_scale * (
        grad_norm
        - jnp.mean(grad_norm, axis=-1, keepdims=True)
        - normed * jnp.mean(grad_norm * normed, axis=-1, keepdims=True)
    )


def gelu_exact(values):
    return jax.nn.gelu(values, approximate=False)


def split_heads(array, first_row, row_count, head_count):
    piece = lax.dynamic_slice_in_dim(array, first_row, row_count, 1)
    return piece.reshape(piece.shape[0], row_count, head_count, piece.shape[2] // head_count)


def block_scores(query_four, key_four):
    return (
        jnp.einsum("sqhd,skhd->shqk", query_four, key_four, preferred_element_type=jnp.float32)
        * score_scale
    )


def softmax_rows(scores, row_max, row_total):
    return jnp.exp(scores - row_max[..., None]) / row_total[..., None]


def score_grads(scores, row_max, row_total, row_delta, grad_four, value_four):
    prob_full = softmax_rows(scores, row_max, row_total)
    prob_grad = jnp.einsum(
        "sqhd,skhd->shqk", grad_four, value_four, preferred_element_type=jnp.float32
    )
    score_low = (prob_full * (prob_grad - row_delta[..., None])).astype(jnp.bfloat16)
    return (prob_full.astype(jnp.bfloat16), score_low)


def body(
    tokens,
    qkv_weight,
    qv_bias,
    out_weight,
    up_weight,
    up_bias,
    down_weight,
    norm_gains,
    row_biases,
    cotangent,
):
    seq_count, local_len, width = tokens.shape
    row_count = seq_count * local_len
    tp_count = lax.axis_size("tp")
    share_len = local_len // tp_count
    share_start = lax.axis_index("tp") * share_len

    def own_rows(array_three):
        return lax.dynamic_slice_in_dim(array_three, share_start, share_len, 1)

    def to_three(array_two):
        return array_two.reshape(seq_count, array_two.shape[0] // seq_count, array_two.shape[1])

    gathered = (
        lax.all_gather(qkv_weight, ("fsdp", "ctx"), axis=0, tiled=True),
        lax.all_gather(out_weight, ("fsdp", "ctx"), axis=0, tiled=True),
        lax.all_gather(up_weight, ("fsdp", "ctx"), axis=0, tiled=True),
        lax.all_gather(down_weight, ("fsdp", "ctx"), axis=0, tiled=True),
        lax.all_gather(norm_gains, ("fsdp", "ctx"), axis=0, tiled=True),
        lax.all_gather(row_biases, ("fsdp", "ctx"), axis=0, tiled=True),
    )
    w_qkv, w_out, w_up, w_down, gains_all, biases_all = gathered
    gains_f = gains_all.astype(jnp.float32)
    biases_f = biases_all.astype(jnp.float32)
    head_width = w_qkv.shape[2]
    head_count = head_width // HD
    flat_tokens = tokens.reshape(row_count, width)
    projected = jnp.dot(
        flat_tokens, w_qkv.reshape(width, 3 * head_width), preferred_element_type=jnp.float32
    )
    projected = projected.reshape(row_count, 3, head_width)
    bias_f = qv_bias.astype(jnp.float32)
    query_low = (projected[:, 0] + bias_f[0]).astype(jnp.bfloat16)
    key_low = projected[:, 1].astype(jnp.bfloat16)
    value_low = (projected[:, 2] + bias_f[1]).astype(jnp.bfloat16)
    keys_full, values_full = (
        lax.all_gather(
            key_low.reshape(seq_count, local_len, head_width), "ctx", axis=1, tiled=True
        ),
        lax.all_gather(
            value_low.reshape(seq_count, local_len, head_width), "ctx", axis=1, tiled=True
        ),
    )
    full_len = keys_full.shape[1]
    block_len = min(512, full_len)
    block_count = full_len // block_len
    query_four = query_low.reshape(seq_count, local_len, head_count, HD)
    stat_shape = (seq_count, head_count, local_len)
    four_shape = (seq_count, local_len, head_count, HD)

    def stats_step(block_idx, running):
        row_max, row_total = running
        scores = block_scores(
            query_four, split_heads(keys_full, block_idx * block_len, block_len, head_count)
        )
        new_max = jnp.maximum(row_max, jnp.max(scores, axis=-1))
        row_total = row_total * jnp.exp(row_max - new_max) + jnp.sum(
            jnp.exp(scores - new_max[..., None]), axis=-1
        )
        return (new_max, row_total)

    row_max, row_total = lax.fori_loop(
        0,
        block_count,
        stats_step,
        (jnp.full(stat_shape, -jnp.inf, jnp.float32), jnp.zeros(stat_shape, jnp.float32)),
    )

    def value_step(block_idx, attn_mixed):
        first_row = block_idx * block_len
        value_four = split_heads(values_full, first_row, block_len, head_count)
        prob_full = softmax_rows(
            block_scores(query_four, split_heads(keys_full, first_row, block_len, head_count)),
            row_max,
            row_total,
        )
        return attn_mixed + jnp.einsum(
            "shqk,skhd->sqhd",
            prob_full.astype(jnp.bfloat16),
            value_four,
            preferred_element_type=jnp.float32,
        )

    zero_four = jnp.zeros(four_shape, jnp.float32)
    attn_mixed = lax.fori_loop(0, block_count, value_step, zero_four)
    mixed_low = attn_mixed.reshape(row_count, head_width).astype(jnp.bfloat16)
    attn_part = contract_last(mixed_low, w_out)
    attn_out = lax.psum(attn_part.astype(jnp.bfloat16), "tp").astype(jnp.float32) + biases_f[:, 0]
    first_out, first_norm, first_scale = norm_forward(
        flat_tokens.astype(jnp.float32) + attn_out, gains_f[:, 0], biases_f[:, 1]
    )
    first_low = first_out.astype(jnp.bfloat16)
    inner_pre = jnp.dot(first_low, w_up, preferred_element_type=jnp.float32) + up_bias.astype(
        jnp.float32
    )
    activated, gelu_back = jax.vjp(gelu_exact, inner_pre)
    act_low = activated.astype(jnp.bfloat16)
    ffn_part = contract_last(act_low, w_down)
    ffn_out = lax.psum(ffn_part.astype(jnp.bfloat16), "tp").astype(jnp.float32) + biases_f[:, 2]
    grad_final = cotangent.reshape(row_count, width).astype(jnp.float32)
    final_out, final_norm, final_scale = norm_forward(
        first_out + ffn_out, gains_f[:, 1], biases_f[:, 3]
    )
    gain2_grad = jnp.sum(grad_final * final_norm, axis=0)
    shift2_grad = jnp.sum(grad_final, axis=0)
    grad_second = norm_backward(grad_final, final_norm, final_scale, gains_f[:, 1])
    ffn_grad_low = grad_second.astype(jnp.bfloat16)
    down_grad = contract_first(ffn_grad_low, act_low)
    down_bias_grad = jnp.sum(ffn_grad_low.astype(jnp.float32), axis=0)
    act_grad = jnp.dot(ffn_grad_low, w_down, preferred_element_type=jnp.float32)
    inner_low = gelu_back(act_grad)[0].astype(jnp.bfloat16)
    up_grad = contract_first(first_low, inner_low)
    up_bias_grad = jnp.sum(inner_low.astype(jnp.float32), axis=0)
    back_part = contract_last(inner_low, w_up)
    first_grad = grad_second + lax.psum(back_part.astype(jnp.bfloat16), "tp").astype(jnp.float32)
    gain1_grad = jnp.sum(first_grad * first_norm, axis=0)
    shift1_grad = jnp.sum(first_grad, axis=0)
    resid_grad = norm_backward(first_grad, first_norm, first_scale, gains_f[:, 0])
    attn_grad_low = resid_grad.astype(jnp.bfloat16)
    out_grad = contract_first(attn_grad_low, mixed_low)
    out_bias_grad = jnp.sum(attn_grad_low.astype(jnp.float32), axis=0)
    mixed_grad_low = jnp.dot(attn_grad_low, w_out, preferred_element_type=jnp.float32).astype(
        jnp.bfloat16
    )
    grad_four = mixed_grad_low.reshape(four_shape)
    row_delta = jnp.einsum(
        "sqhd,sqhd->shq", grad_four.astype(jnp.float32), attn_mixed, precision=highest
    )

    def grad_step(block_idx, running):
        query_grad, key_all, value_all = running
        first_row = block_idx * block_len
        key_four = split_heads(keys_full, first_row, block_len, head_count)
        value_four = split_heads(values_full, first_row, block_len, head_count)
        scores = block_scores(query_four, key_four)
        prob_low, score_low = score_grads(
            scores, row_max, row_total, row_delta, grad_four, value_four
        )
        query_grad = query_grad + jnp.einsum(
            "shqk,skhd->sqhd", score_low, key_four, preferred_element_type=jnp.float32
        )
        key_part = (
            jnp.einsum("shqk,sqhd->skhd", score_low, query_four, preferred_element_type=jnp.float32)
            * score_scale
        )
        value_part = jnp.einsum(
            "shqk,sqhd->skhd", prob_low, grad_four, preferred_element_type=jnp.float32
        )
        key_all = lax.dynamic_update_slice_in_dim(
            key_all, key_part.reshape(seq_count, block_len, head_width), first_row, 1
        )
        value_all = lax.dynamic_update_slice_in_dim(
            value_all, value_part.reshape(seq_count, block_len, head_width), first_row, 1
        )
        return (query_grad, key_all, value_all)

    zeros_full = jnp.zeros((seq_count, full_len, head_width), jnp.float32)
    query_grad, key_all, value_all = lax.fori_loop(
        0, block_count, grad_step, (zero_four, zeros_full, zeros_full)
    )
    key_grad, value_grad = (
        lax.psum_scatter(
            key_all.astype(jnp.bfloat16), "ctx", scatter_dimension=1, tiled=True
        ).astype(jnp.float32),
        lax.psum_scatter(
            value_all.astype(jnp.bfloat16), "ctx", scatter_dimension=1, tiled=True
        ).astype(jnp.float32),
    )
    query_grad_low = (query_grad * score_scale).reshape(row_count, head_width).astype(jnp.bfloat16)
    key_grad_low = key_grad.reshape(row_count, head_width).astype(jnp.bfloat16)
    value_grad_low = value_grad.reshape(row_count, head_width).astype(jnp.bfloat16)
    grad_cat = jnp.stack([query_grad_low, key_grad_low, value_grad_low], axis=1)
    qkv_grad = jnp.einsum("td,tcj->dcj", flat_tokens, grad_cat, preferred_element_type=jnp.float32)
    qv_grad = jnp.stack(
        [
            jnp.sum(query_grad_low.astype(jnp.float32), axis=0),
            jnp.sum(value_grad_low.astype(jnp.float32), axis=0),
        ]
    )
    input_part = contract_last(
        grad_cat.reshape(row_count, 3 * head_width), w_qkv.reshape(width, 3 * head_width)
    )
    gains_grad = jnp.stack([gain1_grad, gain2_grad], axis=1)
    shifts_grad = jnp.stack([shift1_grad, shift2_grad], axis=1)
    tokens_full = resid_grad + lax.psum(input_part.astype(jnp.bfloat16), "tp").astype(jnp.float32)
    tokens_share = own_rows(to_three(tokens_full))
    output_share = own_rows(to_three(final_out))
    biases_grad = jnp.stack(
        [out_bias_grad, shifts_grad[:, 0], down_bias_grad, shifts_grad[:, 1]], axis=1
    )
    shards = (
        lax.psum_scatter(qkv_grad, ("fsdp", "ctx"), scatter_dimension=0, tiled=True),
        lax.psum_scatter(out_grad, ("fsdp", "ctx"), scatter_dimension=0, tiled=True),
        lax.psum_scatter(up_grad, ("fsdp", "ctx"), scatter_dimension=0, tiled=True),
        lax.psum_scatter(down_grad, ("fsdp", "ctx"), scatter_dimension=0, tiled=True),
        lax.psum_scatter(gains_grad, ("fsdp", "ctx"), scatter_dimension=0, tiled=True),
        lax.psum_scatter(biases_grad, ("fsdp", "ctx"), scatter_dimension=0, tiled=True),
    )
    qv_total, up_total = lax.psum((qv_grad, up_bias_grad), ("fsdp", "ctx"))
    output = output_share.astype(jnp.bfloat16)
    tokens_out = tokens_share.astype(jnp.bfloat16)
    return (
        output,
        tokens_out,
        shards[0],
        qv_total,
        shards[1],
        shards[2],
        up_total,
        shards[3],
        shards[4],
        shards[5],
    )


def solution(mesh):
    in_specs = (
        P("fsdp", "ctx", None),
        P(("fsdp", "ctx"), None, "tp"),
        P(None, "tp"),
        P(("fsdp", "ctx"), "tp"),
        P(("fsdp", "ctx"), "tp"),
        P("tp"),
        P(("fsdp", "ctx"), "tp"),
        P(("fsdp", "ctx"), None),
        P(("fsdp", "ctx"), None),
        P("fsdp", "ctx", None),
    )
    out_specs = (
        P("fsdp", ("ctx", "tp"), None),
        P("fsdp", ("ctx", "tp"), None),
        P(("fsdp", "ctx"), None, "tp"),
        P(None, "tp"),
        P(("fsdp", "ctx"), "tp"),
        P(("fsdp", "ctx"), "tp"),
        P("tp"),
        P(("fsdp", "ctx"), "tp"),
        P(("fsdp", "ctx"), None),
        P(("fsdp", "ctx"), None),
    )
    return jax.shard_map(body, mesh=mesh, in_specs=in_specs, out_specs=out_specs, check_vma=False)
```

profile of v0, /device:TPU:0, one launch (start us, length us, event | category | flops | bytes accessed | tf_op | source)
XLA Modules:
  0.0 2090.9 jit_solution(9542823779875088038)
XLA Ops:
  8.0 45.5 %all-gather.8.cloned.1.call-done = bf16[768,3,384]{2,0,1:T(8,128)(2,1)} async-done(((bf16[48,3,384]{2,0,1:T(8,128)(2,1)}), bf16[768,3,384]{2,0,1:T(8,128)(2,1)}) %all-gather.8.cloned.1.call-update) | async-done | bytes 1769488 | tf_op jit(solution)/shard_map/all_gather | solution.py:94
  67.9 53.4 %all_gather.27 = bf16[768,384]{1,0:T(8,128)(2,1)} all-gather(bf16[48,384]{1,0:T(8,128)(2,1)S(1)} %copy-done.33), channel_id=1, replica_groups=mesh['fsdp'=4,'ctx'=4,'tp'=2] {'fsdp','ctx'}, dimensions={0}, use_global_device_ids=true | all-gather | bytes 626688 | tf_op jit(solution)/shard_map/all_gather | solution.py:95
  142.1 48.3 %all-gather.12.cloned.1.call-done = bf16[2,4096,384]{1,2,0:T(8,128)(2,1)} async-done(((bf16[2,1024,384]{1,2,0:T(8,128)(2,1)}), bf16[2,4096,384]{1,2,0:T(8,128)(2,1)}) %all-gather.12.cloned.1.call-update) | async-done | bytes 6291472 | tf_op jit(solution)/shard_map/all_gather | solution.py:116
  190.4 93.1 %while.48 = (s32[]{:T(128)}, f32[2,6,1024]{2,1,0:T(8,128)S(1)}, f32[2,6,1024]{2,1,0:T(8,128)S(1)}, bf16[2,4096,384]{1,2,0:T(8,128)(2,1)}, bf16[2,1024,6,64]{1,3,...) while((s32[]{:T(128)}, f32[2,6,1024]{2,1,0:T(8,128)S(1)}, ...), condition=%wide.region_3.0_spmd.clone, body=%wide.region_0.0_spmd.clone.sunk | while | flops 836825088 | bytes 54902944 | solution.py:141
  283.4 22.7 %all-gather.10.cloned.1.call-done = bf16[2,4096,384]{1,2,0:T(8,128)(2,1)} async-done(((bf16[2,1024,384]{1,2,0:T(8,128)(2,1)}), bf16[2,4096,384]{1,2,0:T(8,128)(2,1)}) %all-gather.10.cloned.1.call-update) | async-done | bytes 6291472 | tf_op jit(solution)/shard_map/all_gather | solution.py:119
  306.2 88.7 %while.49 = (s32[]{:T(128)}, f32[2,1024,6,64]{1,3,2,0:T(8,128)}, bf16[2,4096,384]{1,2,0:T(8,128)(2,1)}, bf16[2,4096,384]{1,2,0:T(8,128)(2,1)}, bf16[2,1024,6,64]...) while((s32[]{:T(128)}, f32[2,1024,6,64]{1,3,2,0:T(8,128)}, ...), condition=%wide.region_5.0_spmd.clone, body=%wide.region_4.0_spmd.clone.sunk | while | flops 1637351424 | bytes 12681393 | solution.py:164
  405.1 29.4 %all-gather.1 = bf16[16,48,2]{1,2,0:T(2,128)(2,1)S(1)} all-gather(bf16[1,48,2]{1,2,0:T(2,128)(2,1)S(1)} %bitcast.191), channel_id=1, replica_groups=mesh['fsdp'=4,'ctx'=4,'tp'=2] {'fsdp','ctx'}, dimensions={0}, use_global_device_ids=true | all-gather | bytes 3264 | tf_op jit(solution)/shard_map/all_gather | solution.py:98
  434.7 29.8 %all-gather = bf16[16,48,4]{1,2,0:T(4,128)(2,1)S(1)} all-gather(bf16[1,48,4]{1,2,0:T(4,128)(2,1)S(1)} %bitcast.190), channel_id=1, replica_groups=mesh['fsdp'=4,'ctx'=4,'tp'=2] {'fsdp','ctx'}, dimensions={0}, use_global_device_ids=true | all-gather | bytes 6528 | tf_op jit(solution)/shard_map/all_gather | solution.py:99
  465.2 22.8 %all-reduce.8.cloned.1.call-done = bf16[2048,768]{1,0:T(8,128)(2,1)} async-done(((bf16[2048,768]{1,0:T(8,128)(2,1)}), bf16[2048,768]{1,0:T(8,128)(2,1)}) %all-reduce.8.cloned.1.call-update) | async-done | bytes 3145744 | tf_op jit(solution)/shard_map/psum | solution.py:167
  496.9 35.6 %all-gather.14.cloned.1.call-done = bf16[768,1536]{1,0:T(8,128)(2,1)} async-done(((bf16[48,1536]{1,0:T(8,128)(2,1)}), bf16[768,1536]{1,0:T(8,128)(2,1)}) %all-gather.14.cloned.1.call-update) | async-done | bytes 2359312 | tf_op jit(solution)/shard_map/all_gather | solution.py:96
  532.5 35.1 %multiply_convert_fusion.1 = (bf16[2048,1536]{1,0:T(8,128)(2,1)}, f32[2048,1536]{1,0:T(8,128)}, f32[2048,1536]{1,0:T(8,128)}) fusion(f32[1536]{0:T(1024)S(1)} %convert_element_type.186, bf16[768,1536]{1,0:T(8,128)(2,1)} %all-gather.14.cloned.1.call-done, f32[2048,768]{1,0:T(8,128)} %subtract_multiply_fusion.2, f32[768]{0:T(1024)S(1)} %get-tuple-element.637, ...), kind=kOutput, calls=%fused_computation.29 | convolution fusion | flops 5044174848 | bytes 40120320 | tf_op jit(solution)/shard_map/dot_general | solution.py:172
  587.0 82.7 %all-reduce.10.cloned.1.call-done = bf16[2048,768]{1,0:T(8,128)(2,1)} async-done(((bf16[2048,768]{1,0:T(8,128)(2,1)}), bf16[2048,768]{1,0:T(8,128)(2,1)}) %all-reduce.10.cloned.1.call-update) | async-done | bytes 3145744 | tf_op jit(solution)/shard_map/psum | solution.py:178
  681.4 18.9 convert_reduce_fusion
  709.4 85.9 %all-reduce.12.cloned.1.call-done = bf16[2048,768]{1,0:T(8,128)(2,1)} async-done(((bf16[2048,768]{1,0:T(8,128)(2,1)}), bf16[2048,768]{1,0:T(8,128)(2,1)}) %all-reduce.12.cloned.1.call-update) | async-done | bytes 3145744 | tf_op jit(solution)/shard_map/psum | solution.py:194
  830.2 482.1 %while.50 = (s32[]{:T(128)}, f32[2,1024,6,64]{1,3,2,0:T(8,128)}, bf16[2,4096,384]{1,2,0:T(8,128)(2,1)}, bf16[2,4096,384]{1,2,0:T(8,128)(2,1)}, bf16[2,4096,384]{...) while((s32[]{:T(128)}, f32[2,1024,6,64]{1,3,2,0:T(8,128)}, ...), condition=%wide.region_18.0_spmd.clone, body=%wide.region_17.0_spmd.clone.sunk | while | flops 4072931328 | bytes 139346160 | solution.py:237
  832.8 12.5 exponential_divide_fusion.2
  845.3 11.2 fusion.106
  856.5 14.5 multiply_convert_fusion.5
  892.2 12.5 exponential_divide_fusion.2
  904.7 11.2 fusion.106
  915.8 14.5 multiply_convert_fusion.5
  952.5 12.5 exponential_divide_fusion.2
  965.0 11.2 fusion.106
  976.1 14.5 multiply_convert_fusion.5
  1012.8 12.5 exponential_divide_fusion.2
  1025.3 11.2 fusion.106
  1036.4 14.5 multiply_convert_fusion.5
  1073.1 12.5 exponential_divide_fusion.2
  1085.6 11.2 fusion.106
  1096.7 14.5 multiply_convert_fusion.5
  1133.4 12.5 exponential_divide_fusion.2
  1145.9 11.2 fusion.106
  1157.1 14.5 multiply_convert_fusion.5
  1193.9 12.5 exponential_divide_fusion.2
  1206.4 11.2 fusion.106
  1217.5 14.5 multiply_convert_fusion.5
  1254.3 12.5 exponential_divide_fusion.2
  1266.8 11.2 fusion.106
  1277.9 14.5 multiply_convert_fusion.5
  1328.0 95.3 %reduce-scatter.12.cloned.1.call-done = bf16[2,1024,384]{1,2,0:T(8,128)(2,1)} async-done(((bf16[2,4096,384]{1,2,0:T(8,128)(2,1)}), bf16[2,1024,384]{1,2,0:T(8,128)(2,1)}) %reduce-scatter.12.cloned.1.call-update) | async-done | bytes 1572880 | tf_op jit(solution)/shard_map/reduce_scatter | solution.py:241
  1425.9 110.9 %reduce-scatter.14.cloned.1.call-done = bf16[2,1024,384]{1,2,0:T(8,128)(2,1)} async-done(((bf16[2,4096,384]{1,2,0:T(8,128)(2,1)}), bf16[2,1024,384]{1,2,0:T(8,128)(2,1)}) %reduce-scatter.14.cloned.1.call-update) | async-done | bytes 1572880 | tf_op jit(solution)/shard_map/reduce_scatter | solution.py:244
  1598.2 57.1 %reduce-scatter.24.cloned.1.call-done = f32[48,4]{1,0:T(8,128)} async-done(((f32[768,4]{1,0:T(8,128)}), f32[48,4]{1,0:T(8,128)}) %reduce-scatter.24.cloned.1.call-update) | async-done | bytes 784
  1656.9 61.1 %all-reduce.1 = (f32[2,384]{1,0:T(2,128)}, f32[1536]{0:T(1024)}) all-reduce(f32[2,384]{1,0:T(2,128)S(1)} %pad_maximum_fusion.5, f32[1536]{0:T(1024)S(1)} %copy-done.43), channel_id=1, replica_groups=mesh['fsdp'=4,'ctx'=4,'tp'=2] {'fsdp','ctx'}, use_global_device_ids=true, to_apply=%region_25.0 | all-reduce | flops 2304 | bytes 18432 | tf_op jit(solution)/shard_map/psum | solution.py:278
  1718.1 58.1 %all-reduce.16.cloned.1.call-done = f32[768,3,384]{2,1,0:T(4,128)} async-done(((f32[768,3,384]{2,1,0:T(4,128)}), f32[768,3,384]{2,1,0:T(4,128)}) %all-reduce.16.cloned.1.call-update) | async-done | bytes 3538960
  1777.8 86.1 %all-reduce.14.cloned.1.call-done = bf16[2048,768]{1,0:T(8,128)(2,1)} async-done(((bf16[2048,768]{1,0:T(8,128)(2,1)}), bf16[2048,768]{1,0:T(8,128)(2,1)}) %all-reduce.14.cloned.1.call-update) | async-done | bytes 3145744 | tf_op jit(solution)/shard_map/psum | solution.py:264
  1869.6 56.6 %reduce-scatter.16.cloned.1.call-done = f32[48,384]{1,0:T(8,128)} async-done(((f32[768,384]{1,0:T(8,128)}), f32[48,384]{1,0:T(8,128)}) %reduce-scatter.16.cloned.1.call-update) | async-done | bytes 73744 | tf_op jit(solution)/shard_map/reduce_scatter | solution.py:272
  1926.2 78.9 %reduce-scatter.20.cloned.1.call-done = f32[48,1536]{1,0:T(8,128)} async-done(((f32[768,1536]{1,0:T(8,128)}), f32[48,1536]{1,0:T(8,128)}) %reduce-scatter.20.cloned.1.call-update) | async-done | bytes 294928 | tf_op jit(solution)/shard_map/reduce_scatter | solution.py:274
  2005.0 79.2 %reduce-scatter.18.cloned.1.call-done = f32[48,1536]{1,0:T(8,128)} async-done(((f32[768,1536]{1,0:T(8,128)}), f32[48,1536]{1,0:T(8,128)}) %reduce-scatter.18.cloned.1.call-update) | async-done | bytes 294928 | tf_op jit(solution)/shard_map/reduce_scatter | solution.py:273
  (344 shorter events, 575.8 us)
Async XLA Ops:
  7.2 46.2 %all-gather.8.cloned.1.call-start = ((), (), s32[]{:S(2)}) async-start(), calls=%async_computation.7 | async-start | bytes 1880064 | tf_op jit(solution)/shard_map/all_gather | solution.py:94
  7.9 182.5 %all-gather.12.cloned.1.call-start = ((), (), s32[]{:S(2)}) async-start(), calls=%async_computation.9 | async-start | bytes 7864320 | tf_op jit(solution)/shard_map/all_gather | solution.py:116
  67.7 238.5 %all-gather.10.cloned.1.call-start = ((), (), s32[]{:S(2)}) async-start(), calls=%async_computation.8 | async-start | bytes 7864320 | tf_op jit(solution)/shard_map/all_gather | solution.py:119
  141.9 346.1 %all-reduce.8.cloned.1.call-start = ((), (), s32[]{:S(2)}) async-start(), calls=%async_computation.10 | async-start | bytes 6291456 | tf_op jit(solution)/shard_map/psum | solution.py:167
  394.9 8.9 copy-start.12
  394.9 9.0 copy-start.21
  400.4 34.3 %copy-start.46 = (bf16[48,4]{0,1:T(4,128)(2,1)S(1)}, bf16[48,4]{0,1:T(4,128)(2,1)}, u32[]{:S(2)}) copy-start(bf16[48,4]{0,1:T(4,128)(2,1)} %param.24) | copy-start | bytes 1156
  400.4 87.7 %copy-start.7 = (bf16[2,1024,768]{2,1,0:T(8,128)(2,1)S(1)}, bf16[2,1024,768]{2,1,0:T(8,128)(2,1)}, u32[]{:S(2)}) copy-start(bf16[2,1024,768]{2,1,0:T(8,128)(2,1)} %param.16) | copy-start | bytes 9437188
  403.9 128.7 %all-gather.14.cloned.1.call-start = ((), (), s32[]{:S(2)}) async-start(), calls=%async_computation.11 | async-start | bytes 2506752 | tf_op jit(solution)/shard_map/all_gather | solution.py:96
  404.4 171.3 %all-gather.16.cloned.1.call-start = ((), (), s32[]{:S(2)}) async-start(), calls=%async_computation.12 | async-start | bytes 2506752 | tf_op jit(solution)/shard_map/all_gather | solution.py:97
  405.0 264.7 %all-reduce.10.cloned.1.call-start = ((), (), s32[]{:S(2)}) async-start(), calls=%async_computation.13 | async-start | bytes 6291456 | tf_op jit(solution)/shard_map/psum | solution.py:178
  434.6 244.5 %copy-start.27 = (f32[768]{0:T(1024)}, f32[768]{0:T(1024)S(1)}, u32[]{:S(2)}) copy-start(f32[768]{0:T(1024)S(1)} %get-tuple-element.639) | copy-start | bytes 9220
  434.7 370.4 %copy-start.31 = (f32[768]{0:T(1024)}, f32[768]{0:T(1024)S(1)}, u32[]{:S(2)}) copy-start(f32[768]{0:T(1024)S(1)} %get-tuple-element.640) | copy-start | bytes 9220
  465.2 204.5 %copy-start.35 = (f32[768]{0:T(1024)}, f32[768]{0:T(1024)S(1)}, u32[]{:S(2)}) copy-start(f32[768]{0:T(1024)S(1)} %get-tuple-element.637) | copy-start | bytes 9220
  575.8 9.3 copy-start.5
  585.0 210.3 %all-reduce.12.cloned.1.call-start = ((), (), s32[]{:S(2)}) async-start(), calls=%async_computation.14 | async-start | bytes 6291456 | tf_op jit(solution)/shard_map/psum | solution.py:194
  681.4 18.9 copy-start.4
  709.3 713.9 %reduce-scatter.12.cloned.1.call-start = ((), (), s32[]{:S(2)}) async-start(), calls=%async_computation.15 | async-start | bytes 7864320 | tf_op jit(solution)/shard_map/reduce_scatter | solution.py:241
  709.4 95.6 %copy-start.30 = (f32[2048]{0:T(1024)S(1)}, f32[2048]{0:T(1024)}, u32[]{:S(2)}) copy-start(f32[2048]{0:T(1024)} %copy-done.29) | copy-start | bytes 24580
  795.3 9.7 copy-start.11
  805.0 8.9 copy-start.19
  879.9 8.6 copy-start.3
  939.3 9.5 copy-start.3
  999.6 9.5 copy-start.3
  1059.9 9.5 copy-start.3
  1120.2 9.5 copy-start.3
  1180.5 9.5 copy-start.3
  1241.0 9.5 copy-start.3
  1301.4 9.5 copy-start.3
  1312.3 224.4 %reduce-scatter.14.cloned.1.call-start = ((), (), s32[]{:S(2)}) async-start(), calls=%async_computation.16 | async-start | bytes 7864320 | tf_op jit(solution)/shard_map/reduce_scatter | solution.py:244
  1312.9 283.8 %reduce-scatter.22.cloned.1.call-start = ((), (), s32[]{:S(2)}) async-start(), calls=%async_computation.21 | async-start | bytes 417792
  1315.6 339.6 %reduce-scatter.24.cloned.1.call-start = ((), (), s32[]{:S(2)}) async-start(), calls=%async_computation.22 | async-start | bytes 417792
  1321.4 217.9 %copy-start.8 = (bf16[2,1024,768]{2,1,0:T(8,128)(2,1)S(1)}, bf16[2,1024,768]{2,1,0:T(8,128)(2,1)}, u32[]{:S(2)}) copy-start(bf16[2,1024,768]{2,1,0:T(8,128)(2,1)} %param.16) | copy-start | bytes 9437188
  1327.9 448.2 %all-reduce.16.cloned.1.call-start = ((), (), s32[]{:S(2)}) async-start(), calls=%async_computation.23 | async-start | bytes 9437184
  1553.8 8.9 copy-start.17
  1553.8 310.0 %all-reduce.14.cloned.1.call-start = ((), (), s32[]{:S(2)}) async-start(), calls=%async_computation.17 | async-start | bytes 6291456 | tf_op jit(solution)/shard_map/psum | solution.py:264
  1562.5 363.6 %reduce-scatter.16.cloned.1.call-start = ((), (), s32[]{:S(2)}) async-start(), calls=%async_computation.18 | async-start | bytes 1253376 | tf_op jit(solution)/shard_map/reduce_scatter | solution.py:272
  1568.4 10.6 copy-start.32
  1568.4 10.6 copy-start.36
  1568.4 436.6 %reduce-scatter.20.cloned.1.call-start = ((), (), s32[]{:S(2)}) async-start(), calls=%async_computation.20 | async-start | bytes 5013504 | tf_op jit(solution)/shard_map/reduce_scatter | solution.py:274
  1579.0 10.7 copy-start.48
  1579.0 11.9 copy-start.24
  1579.0 11.9 copy-start.26
  1579.0 11.9 copy-start.28
  1579.0 11.9 copy-start.34
  1579.0 505.2 %reduce-scatter.18.cloned.1.call-start = ((), (), s32[]{:S(2)}) async-start(), calls=%async_computation.19 | async-start | bytes 5013504 | tf_op jit(solution)/shard_map/reduce_scatter | solution.py:273
  1590.9 65.7 %copy-start.15 = (bf16[2,1024,384]{1,2,0:T(8,128)(2,1)S(1)}, bf16[2,1024,384]{1,2,0:T(8,128)(2,1)}, u32[]{:S(2)}) copy-start(bf16[2,1024,384]{1,2,0:T(8,128)(2,1)} %reduce-scatter.14.cloned.1.call-done) | copy-start | bytes 4718596
  1590.9 66.0 %copy-start.43 = (f32[1536]{0:T(1024)S(1)}, f32[1536]{0:T(1024)}, u32[]{:S(2)}) copy-start(f32[1536]{0:T(1024)} %get-tuple-element.708) | copy-start | bytes 18436
  (25 other events, 79.5 us)
Sparse Core Ops, SparseCore 0:
  10.2 43.1 all-gather.7
  67.8 122.5 all-gather.11
  192.5 113.6 all-gather.9
  404.0 83.9 all-reduce.7
  490.2 42.3 all-gather.13
  534.7 41.0 all-gather.15
  585.1 84.5 all-reduce.9
  709.5 85.8 all-reduce.11
  1312.5 110.7 reduce-scatter.11
  1425.4 111.2 reduce-scatter.13
  1540.2 56.4 reduce-scatter.21
  1600.1 55.0 reduce-scatter.23
  1658.8 117.2 all-reduce.15
  1778.3 85.5 all-reduce.13
  1867.9 58.1 reduce-scatter.15
  1930.4 74.5 reduce-scatter.19
  2009.3 74.8 reduce-scatter.17
where the time goes:
time: 2100 us; the launch traced here: 2090 us
  waiting for transfers between devices  977 us (47%)
  matrix products  697 us (33%)
  blocking collectives  174 us (8%)
  local copies, waits for them, and re-layouts  134 us (6%)
  other arithmetic  92 us (4%)
    dot_general x16, matrix products, block_scores(): jnp.einsum('sqhd,skhd->shqk', query_four, key_four, preferred_element_typ...  141 us
    unnamed x20, waiting for transfers between devices  119 us
    dot_general x8, matrix products, score_grads(): jnp.einsum('sqhd,skhd->shqk', grad_four, value_four, preferred_element_ty...  116 us
    reduce_scatter x1, waiting for transfers between devices, body(): lax.psum_scatter(value_all.astype(jnp.bfloat16), 'ctx', scatter_dimension...  111 us
    reduce_scatter x1, waiting for transfers between devices, body(): lax.psum_scatter(key_all.astype(jnp.bfloat16), 'ctx', scatter_dimension=1...  95.3 us
    dot_general x8, matrix products, grad_step(): jnp.einsum('shqk,sqhd->skhd', prob_low, grad_four, preferred_element_type...  89.2 us
    psum x1, waiting for transfers between devices, body(): lax.psum(input_part.astype(jnp.bfloat16), 'tp').astype(jnp.float32)  86.1 us
    psum x1, waiting for transfers between devices, body(): lax.psum(back_part.astype(jnp.bfloat16), 'tp').astype(jnp.float32)  85.9 us
  transfers between devices with their start and end apart: 17, of which 17 were waited for; matrix products, arithmetic and copies ran while one was open for 12% of the time, Pallas kernels for 0%

commit v1 on v0

--- a/solution.py
+++ b/solution.py
@@ -7,6 +7,28 @@
 epsilon = 1e-12
 score_scale = 0.125
 highest = lax.Precision.HIGHEST
+
+
+def in_order(blocks, dim):
+    shape = list(blocks.shape[1:])
+    shape[dim] *= blocks.shape[0]
+    return jnp.moveaxis(blocks, 0, dim).reshape(shape)
+
+
+def ring_gather(value, axis, dim):
+    devices = lax.axis_size(axis)
+    pairs = [(i, (i + 1) % devices) for i in range(devices)]
+    back = [(b, a) for a, b in pairs]
+    lower, upper = ([], [])
+    for turn in range(devices - 1):
+        if turn % 2 == 0:
+            lower.append(lax.ppermute(lower[-1] if lower else value, axis, pairs))
+        else:
+            upper.append(lax.ppermute(upper[-1] if upper else value, axis, back))
+    blocks = jnp.stack([*lower[::-1], value, *upper])
+    shift = lax.axis_index(axis) - len(lower)
+    blocks = blocks[(jnp.arange(devices) - shift) % devices]
+    return in_order(blocks, dim)
 
 
 def contract_last(left, right):
@@ -91,7 +113,7 @@
         return array_two.reshape(seq_count, array_two.shape[0] // seq_count, array_two.shape[1])
 
     gathered = (
-        lax.all_gather(qkv_weight, ("fsdp", "ctx"), axis=0, tiled=True),
+        ring_gather(qkv_weight, ("fsdp", "ctx"), 0),
         lax.all_gather(out_weight, ("fsdp", "ctx"), axis=0, tiled=True),
         lax.all_gather(up_weight, ("fsdp", "ctx"), axis=0, tiled=True),
         lax.all_gather(down_weight, ("fsdp", "ctx"), axis=0, tiled=True),

time: 2100 us -> 1960 us (0.933)
  waiting for transfers between devices: 977 us -> 696 us
  other arithmetic: 92 us -> 143 us
  starting transfers between devices: 1.44 us -> 34.8 us
  local copies, waits for them, and re-layouts: 134 us -> 163 us
  matrix products: 697 us -> 725 us
    reduce_scatter x1, waiting for transfers between devices: 56.6 us -> 0.01 us  [body(): lax.psum_scatter(out_grad, ('fsdp', 'ctx'), scatter_dimension=0, tiled=True)]
    unnamed x20 -> x19, waiting for transfers between devices: 119 us -> 62.1 us
    reduce_sum x8, other arithmetic: 34.4 us -> 83.8 us  [stats_step(): jnp.sum(jnp.exp(scores - new_max[..., None]), axis=-1)]
    reduce_scatter x1, waiting for transfers between devices: 78.9 us -> 31.9 us  [body(): lax.psum_scatter(down_grad, ('fsdp', 'ctx'), scatter_dimension=0, tiled=T...]
    psum x1, waiting for transfers between devices: 86.1 us -> 39.4 us  [body(): lax.psum(input_part.astype(jnp.bfloat16), 'tp').astype(jnp.float32)]
    all_gather x1 -> x0, waiting for transfers between devices: 45.5 us -> none  [body(): lax.all_gather(qkv_weight, ('fsdp', 'ctx'), axis=0, tiled=True)]
    dot_general x16, matrix products: 141 us -> 181 us  [block_scores(): jnp.einsum('sqhd,skhd->shqk', query_four, key_four, preferred_element_typ...]
    unnamed x107 -> x135, local copies, waits for them, and re-layouts: 17.4 us -> 54.3 us
  transfers between devices with their start and end apart: 17 -> 31, of which waited for: 17 -> 21; matrix products, arithmetic and copies ran while one was open for 12% -> 18% of each run, Pallas kernels for 0% -> 0%
where the time goes in v1:
time: 1960 us; the launch traced here: 1950 us
  matrix products  725 us (37%)
  waiting for transfers between devices  696 us (36%)
  blocking collectives  170 us (9%)
  local copies, waits for them, and re-layouts  163 us (8%)
  other arithmetic  143 us (7%)
  starting transfers between devices  34.8 us (2%)
    dot_general x16, matrix products, block_scores(): jnp.einsum('sqhd,skhd->shqk', query_four, key_four, preferred_element_typ...  181 us
    dot_general x8, matrix products, score_grads(): jnp.einsum('sqhd,skhd->shqk', grad_four, value_four, preferred_element_ty...  116 us
    reduce_scatter x1, waiting for transfers between devices, body(): lax.psum_scatter(value_all.astype(jnp.bfloat16), 'ctx', scatter_dimension...  108 us
    reduce_scatter x1, waiting for transfers between devices, body(): lax.psum_scatter(key_all.astype(jnp.bfloat16), 'ctx', scatter_dimension=1...  103 us
    psum x1, waiting for transfers between devices, body(): lax.psum(back_part.astype(jnp.bfloat16), 'tp').astype(jnp.float32)  85.7 us
    reduce_sum x8, other arithmetic, stats_step(): jnp.sum(jnp.exp(scores - new_max[..., None]), axis=-1)  83.8 us
    psum x1, waiting for transfers between devices, body(): lax.psum(ffn_part.astype(jnp.bfloat16), 'tp').astype(jnp.float32)  83.5 us
    dot_general x8, matrix products, grad_step(): jnp.einsum('shqk,sqhd->skhd', prob_low, grad_four, preferred_element_type...  82.4 us
  transfers between devices with their start and end apart: 31, of which 21 were waited for; matrix products, arithmetic and copies ran while one was open for 18% of the time, Pallas kernels for 0%

profile of v1, /device:TPU:0, one launch (start us, length us, event | category | flops | bytes accessed | tf_op | source)
XLA Modules:
  0.0 1950.7 jit_solution(18260021035707292565)
XLA Ops:
  96.0 48.8 %all_gather.23 = bf16[768,384]{1,0:T(8,128)(2,1)} all-gather(bf16[48,384]{1,0:T(8,128)(2,1)S(1)} %copy-done.35), channel_id=1, replica_groups=mesh['fsdp'=4,'ctx'=4,'tp'=2] {'fsdp','ctx'}, dimensions={0}, use_global_device_ids=true | all-gather | bytes 626688 | tf_op jit(solution)/shard_map/all_gather | solution.py:117
  164.1 52.5 %all-gather.9.cloned.1.call-done = bf16[2,4096,384]{2,1,0:T(8,128)(2,1)} async-done(((bf16[2,1024,384]{2,1,0:T(8,128)(2,1)}), bf16[2,4096,384]{2,1,0:T(8,128)(2,1)}) %all-gather.9.cloned.1.call-update) | async-done | bytes 6291472 | tf_op jit(solution)/shard_map/all_gather | solution.py:138
  225.2 175.3 %while.48 = (s32[]{:T(128)}, f32[2,6,1024]{2,1,0:T(8,128)S(1)}, f32[2,6,1024]{2,1,0:T(8,128)S(1)}, bf16[2,4096,384]{1,2,0:T(8,128)(2,1)}, bf16[2,1024,6,64]{1,3,...) while((s32[]{:T(128)}, f32[2,6,1024]{2,1,0:T(8,128)S(1)}, ...), condition=%wide.region_3.4_spmd.clone, body=%wide.region_0.3_spmd.clone.sunk | while | flops 836825088 | bytes 54902936 | solution.py:163
  236.7 10.5 fusion.93
  258.6 10.6 fusion.93
  280.7 10.5 fusion.93
  302.7 10.4 fusion.93
  324.5 10.4 fusion.93
  346.3 10.4 fusion.93
  368.2 10.4 fusion.93
  390.0 10.4 fusion.93
  409.4 85.8 %while.49 = (s32[]{:T(128)}, f32[2,1024,6,64]{1,3,2,0:T(8,128)}, bf16[2,4096,384]{1,2,0:T(8,128)(2,1)}, bf16[2,4096,384]{1,2,0:T(8,128)(2,1)}, bf16[2,1024,6,64]...) while((s32[]{:T(128)}, f32[2,1024,6,64]{1,3,2,0:T(8,128)}, ...), condition=%wide.region_5.6_spmd.clone, body=%wide.region_4.5_spmd.clone.sunk | while | flops 1637351424 | bytes 12681385 | solution.py:186
  506.0 30.9 %all-gather = bf16[16,48,4]{1,2,0:T(4,128)(2,1)S(1)} all-gather(bf16[1,48,4]{1,2,0:T(4,128)(2,1)S(1)} %bitcast.229), channel_id=1, replica_groups=mesh['fsdp'=4,'ctx'=4,'tp'=2] {'fsdp','ctx'}, dimensions={0}, use_global_device_ids=true | all-gather | bytes 6528 | tf_op jit(solution)/shard_map/all_gather | solution.py:121
  537.6 28.7 %all-gather.1 = bf16[16,48,2]{1,2,0:T(2,128)(2,1)S(1)} all-gather(bf16[1,48,2]{1,2,0:T(2,128)(2,1)S(1)} %bitcast.230), channel_id=1, replica_groups=mesh['fsdp'=4,'ctx'=4,'tp'=2] {'fsdp','ctx'}, dimensions={0}, use_global_device_ids=true | all-gather | bytes 3264 | tf_op jit(solution)/shard_map/all_gather | solution.py:120
  566.5 23.5 %all-reduce.8.cloned.1.call-done = bf16[2048,768]{1,0:T(8,128)(2,1)} async-done(((bf16[2048,768]{1,0:T(8,128)(2,1)}), bf16[2048,768]{1,0:T(8,128)(2,1)}) %all-reduce.8.cloned.1.call-update) | async-done | bytes 3145744 | tf_op jit(solution)/shard_map/psum | solution.py:189
  600.3 35.1 %multiply_convert_fusion.1 = (bf16[2048,1536]{1,0:T(8,128)(2,1)}, f32[2048,1536]{1,0:T(8,128)}, f32[2048,1536]{1,0:T(8,128)}) fusion(f32[1536]{0:T(1024)S(1)} %convert_element_type.186, bf16[768,1536]{1,0:T(8,128)(2,1)} %all-gather.11.cloned.1.call-done, f32[2048,768]{1,0:T(8,128)} %subtract_multiply_fusion.2, f32[768]{0:T(1024)S(1)} %get-tuple-element.637, ...), kind=kOutput, calls=%fused_computation.30 | convolution fusion | flops 5044174848 | bytes 40120320 | tf_op jit(solution)/shard_map/dot_general | solution.py:194
  647.0 83.5 %all-reduce.10.cloned.1.call-done = bf16[2048,768]{1,0:T(8,128)(2,1)} async-done(((bf16[2048,768]{1,0:T(8,128)(2,1)}), bf16[2048,768]{1,0:T(8,128)(2,1)}) %all-reduce.10.cloned.1.call-update) | async-done | bytes 3145744 | tf_op jit(solution)/shard_map/psum | solution.py:200
  741.9 18.8 convert_reduce_fusion
  770.1 85.7 %all-reduce.12.cloned.1.call-done = bf16[2048,768]{1,0:T(8,128)(2,1)} async-done(((bf16[2048,768]{1,0:T(8,128)(2,1)}), bf16[2048,768]{1,0:T(8,128)(2,1)}) %all-reduce.12.cloned.1.call-update) | async-done | bytes 3145744 | tf_op jit(solution)/shard_map/psum | solution.py:216
  890.5 474.8 %while.50 = (s32[]{:T(128)}, f32[2,1024,6,64]{1,3,2,0:T(8,128)}, bf16[2,4096,384]{1,2,0:T(8,128)(2,1)}, bf16[2,4096,384]{1,2,0:T(8,128)(2,1)}, bf16[2,4096,384]{...) while((s32[]{:T(128)}, f32[2,1024,6,64]{1,3,2,0:T(8,128)}, ...), condition=%wide.region_18.19_spmd.clone, body=%wide.region_17.18_spmd.clone.sunk | while | flops 4072931328 | bytes 136200400 | solution.py:259
  891.9 12.5 exponential_divide_fusion.2
  905.6 14.5 multiply_convert_fusion.5
  950.3 12.6 exponential_divide_fusion.2
  964.1 14.5 multiply_convert_fusion.5
  987.5 10.3 fusion.108
  1009.8 12.6 exponential_divide_fusion.2
  1023.5 14.5 multiply_convert_fusion.5
  1069.2 12.5 exponential_divide_fusion.2
  1082.9 14.5 multiply_convert_fusion.5
  1106.3 10.3 fusion.108
  1128.6 12.6 exponential_divide_fusion.2
  1142.3 14.5 multiply_convert_fusion.5
  1165.8 10.3 fusion.108
  1188.0 12.5 exponential_divide_fusion.2
  1201.7 14.5 multiply_convert_fusion.5
  1247.5 12.5 exponential_divide_fusion.2
  1261.3 14.5 multiply_convert_fusion.5
  1307.0 12.5 exponential_divide_fusion.2
  1320.7 14.5 multiply_convert_fusion.5
  1373.2 103.0 %reduce-scatter.12.cloned.1.call-done = bf16[2,1024,384]{1,2,0:T(8,128)(2,1)} async-done(((bf16[2,4096,384]{1,2,0:T(8,128)(2,1)}), bf16[2,1024,384]{1,2,0:T(8,128)(2,1)}) %reduce-scatter.12.cloned.1.call-update) | async-done | bytes 1572880 | tf_op jit(solution)/shard_map/reduce_scatter | solution.py:263
  1481.7 108.2 %reduce-scatter.14.cloned.1.call-done = bf16[2,1024,384]{1,2,0:T(8,128)(2,1)} async-done(((bf16[2,4096,384]{1,2,0:T(8,128)(2,1)}), bf16[2,1024,384]{1,2,0:T(8,128)(2,1)}) %reduce-scatter.14.cloned.1.call-update) | async-done | bytes 1572880 | tf_op jit(solution)/shard_map/reduce_scatter | solution.py:266
  1632.3 10.6 fusion.33
  1643.1 10.6 fusion.24
  1661.4 60.2 %reduce-scatter.24.cloned.1.call-done = f32[48,4]{1,0:T(8,128)} async-done(((f32[768,4]{1,0:T(8,128)}), f32[48,4]{1,0:T(8,128)}) %reduce-scatter.24.cloned.1.call-update) | async-done | bytes 784
  1723.2 61.8 %all-reduce.1 = (f32[2,384]{1,0:T(2,128)}, f32[1536]{0:T(1024)}) all-reduce(f32[2,384]{1,0:T(2,128)S(1)} %pad_maximum_fusion.2, f32[1536]{0:T(1024)S(1)} %copy-done.45), channel_id=1, replica_groups=mesh['fsdp'=4,'ctx'=4,'tp'=2] {'fsdp','ctx'}, use_global_device_ids=true, to_apply=%region_25.26 | all-reduce | flops 2304 | bytes 18432 | tf_op jit(solution)/shard_map/psum | solution.py:300
  1786.8 39.4 %all-reduce.14.cloned.1.call-done = bf16[2048,768]{1,0:T(8,128)(2,1)} async-done(((bf16[2048,768]{1,0:T(8,128)(2,1)}), bf16[2048,768]{1,0:T(8,128)(2,1)}) %all-reduce.14.cloned.1.call-update) | async-done | bytes 3145744 | tf_op jit(solution)/shard_map/psum | solution.py:286
  1831.9 31.9 %reduce-scatter.20.cloned.1.call-done = f32[48,1536]{1,0:T(8,128)} async-done(((f32[768,1536]{1,0:T(8,128)}), f32[48,1536]{1,0:T(8,128)}) %reduce-scatter.20.cloned.1.call-update) | async-done | bytes 294928 | tf_op jit(solution)/shard_map/reduce_scatter | solution.py:296
  1863.8 79.1 %reduce-scatter.18.cloned.1.call-done = f32[48,1536]{1,0:T(8,128)} async-done(((f32[768,1536]{1,0:T(8,128)}), f32[48,1536]{1,0:T(8,128)}) %reduce-scatter.18.cloned.1.call-update) | async-done | bytes 294928 | tf_op jit(solution)/shard_map/reduce_scatter | solution.py:295
  (386 shorter events, 688.3 us)
Async XLA Ops:
  8.0 208.6 %all-gather.9.cloned.1.call-start = ((), (), s32[]{:S(2)}) async-start(), calls=%async_computation.8 | async-start | bytes 7864320 | tf_op jit(solution)/shard_map/all_gather | solution.py:138
  8.1 8.5 collective-permute-start
  16.5 7.9 collective-permute-start.1
  16.5 7.9 collective-permute-start.8
  24.4 8.1 collective-permute-start.2
  24.4 8.1 collective-permute-start.9
  32.5 8.1 collective-permute-start.3
  32.6 8.1 collective-permute-start.10
  40.6 7.0 collective-permute-start.4
  40.7 7.8 collective-permute-start.11
  47.6 7.0 collective-permute-start.5
  48.4 8.0 collective-permute-start.12
  54.6 7.0 collective-permute-start.6
  56.4 7.0 collective-permute-start.13
  61.6 6.9 collective-permute-start.7
  63.4 15.8 collective-permute-start.14
  95.8 304.8 %all-gather.7.cloned.1.call-start = ((), (), s32[]{:S(2)}) async-start(), calls=%async_computation.7 | async-start | bytes 7864320 | tf_op jit(solution)/shard_map/all_gather | solution.py:141
  164.0 426.0 %all-reduce.8.cloned.1.call-start = ((), (), s32[]{:S(2)}) async-start(), calls=%async_computation.9 | async-start | bytes 6291456 | tf_op jit(solution)/shard_map/psum | solution.py:189
  501.2 36.5 %copy-start.49 = (bf16[48,2]{0,1:T(2,128)(2,1)S(1)}, bf16[48,2]{0,1:T(2,128)(2,1)}, u32[]{:S(2)}) copy-start(bf16[48,2]{0,1:T(2,128)(2,1)} %param.23) | copy-start | bytes 580
  501.2 65.3 %copy-start.46 = (bf16[1536]{0:T(1024)(128)(2,1)S(1)}, bf16[1536]{0:T(1024)(128)(2,1)}, u32[]{:S(2)}) copy-start(bf16[1536]{0:T(1024)(128)(2,1)} %param.21) | copy-start | bytes 9220
  504.7 89.4 %copy-start.8 = (bf16[2,1024,768]{2,1,0:T(8,128)(2,1)S(1)}, bf16[2,1024,768]{2,1,0:T(8,128)(2,1)}, u32[]{:S(2)}) copy-start(bf16[2,1024,768]{2,1,0:T(8,128)(2,1)} %param.16) | copy-start | bytes 9437188
  504.8 95.5 %all-gather.11.cloned.1.call-start = ((), (), s32[]{:S(2)}) async-start(), calls=%async_computation.10 | async-start | bytes 2506752 | tf_op jit(solution)/shard_map/all_gather | solution.py:118
  505.3 130.1 %all-gather.13.cloned.1.call-start = ((), (), s32[]{:S(2)}) async-start(), calls=%async_computation.11 | async-start | bytes 2506752 | tf_op jit(solution)/shard_map/all_gather | solution.py:119
  505.9 224.6 %all-reduce.10.cloned.1.call-start = ((), (), s32[]{:S(2)}) async-start(), calls=%async_computation.12 | async-start | bytes 6291456 | tf_op jit(solution)/shard_map/psum | solution.py:200
  537.6 192.9 %copy-start.37 = (f32[768]{0:T(1024)}, f32[768]{0:T(1024)S(1)}, u32[]{:S(2)}) copy-start(f32[768]{0:T(1024)S(1)} %get-tuple-element.637) | copy-start | bytes 9220
  566.5 173.2 %copy-start.29 = (f32[768]{0:T(1024)}, f32[768]{0:T(1024)S(1)}, u32[]{:S(2)}) copy-start(f32[768]{0:T(1024)S(1)} %get-tuple-element.639) | copy-start | bytes 9220
  566.5 298.7 %copy-start.33 = (f32[768]{0:T(1024)}, f32[768]{0:T(1024)S(1)}, u32[]{:S(2)}) copy-start(f32[768]{0:T(1024)S(1)} %get-tuple-element.640) | copy-start | bytes 9220
  644.6 211.2 %all-reduce.12.cloned.1.call-start = ((), (), s32[]{:S(2)}) async-start(), calls=%async_computation.13 | async-start | bytes 6291456 | tf_op jit(solution)/shard_map/psum | solution.py:216
  741.9 18.9 copy-start.3
  769.9 706.4 %reduce-scatter.12.cloned.1.call-start = ((), (), s32[]{:S(2)}) async-start(), calls=%async_computation.14 | async-start | bytes 7864320 | tf_op jit(solution)/shard_map/reduce_scatter | solution.py:263
  770.1 95.1 %copy-start.32 = (f32[2048]{0:T(1024)S(1)}, f32[2048]{0:T(1024)}, u32[]{:S(2)}) copy-start(f32[2048]{0:T(1024)} %copy-done.31) | copy-start | bytes 24580
  1365.3 224.6 %reduce-scatter.14.cloned.1.call-start = ((), (), s32[]{:S(2)}) async-start(), calls=%async_computation.15 | async-start | bytes 7864320 | tf_op jit(solution)/shard_map/reduce_scatter | solution.py:266
  1366.1 293.9 %reduce-scatter.22.cloned.1.call-start = ((), (), s32[]{:S(2)}) async-start(), calls=%async_computation.20 | async-start | bytes 417792
  1372.1 349.4 %reduce-scatter.24.cloned.1.call-start = ((), (), s32[]{:S(2)}) async-start(), calls=%async_computation.21 | async-start | bytes 417792
  1373.2 411.9 %all-reduce.16.cloned.1.call-start = ((), (), s32[]{:S(2)}) async-start(), calls=%async_computation.22 | async-start | bytes 9437184
  1481.7 121.8 %copy-start.9 = (bf16[2,1024,768]{2,1,0:T(8,128)(2,1)S(1)}, bf16[2,1024,768]{2,1,0:T(8,128)(2,1)}, u32[]{:S(2)}) copy-start(bf16[2,1024,768]{2,1,0:T(8,128)(2,1)} %param.16) | copy-start | bytes 9437188
  1617.8 208.4 %all-reduce.14.cloned.1.call-start = ((), (), s32[]{:S(2)}) async-start(), calls=%async_computation.16 | async-start | bytes 6291456 | tf_op jit(solution)/shard_map/psum | solution.py:286
  1626.4 205.4 %reduce-scatter.16.cloned.1.call-start = ((), (), s32[]{:S(2)}) async-start(), calls=%async_computation.17 | async-start | bytes 1253376 | tf_op jit(solution)/shard_map/reduce_scatter | solution.py:294
  1632.2 10.8 copy-start.34
  1632.2 10.8 copy-start.38
  1632.3 231.5 %reduce-scatter.20.cloned.1.call-start = ((), (), s32[]{:S(2)}) async-start(), calls=%async_computation.19 | async-start | bytes 5013504 | tf_op jit(solution)/shard_map/reduce_scatter | solution.py:296
  1643.0 12.0 copy-start.26
  1643.0 12.0 copy-start.28
  1643.0 12.0 copy-start.30
  1643.0 12.0 copy-start.36
  1643.0 299.9 %reduce-scatter.18.cloned.1.call-start = ((), (), s32[]{:S(2)}) async-start(), calls=%async_computation.18 | async-start | bytes 5013504 | tf_op jit(solution)/shard_map/reduce_scatter | solution.py:295
  1655.0 67.9 %copy-start.16 = (bf16[2,1024,384]{1,2,0:T(8,128)(2,1)S(1)}, bf16[2,1024,384]{1,2,0:T(8,128)(2,1)}, u32[]{:S(2)}) copy-start(bf16[2,1024,384]{1,2,0:T(8,128)(2,1)} %reduce-scatter.14.cloned.1.call-done) | copy-start | bytes 4718596
  1655.0 68.2 %copy-start.45 = (f32[1536]{0:T(1024)S(1)}, f32[1536]{0:T(1024)}, u32[]{:S(2)}) copy-start(f32[1536]{0:T(1024)} %get-tuple-element.708) | copy-start | bytes 18436
  (34 other events, 169.5 us)
Sparse Core Ops, SparseCore 0:
  95.9 120.6 all-gather.8
  218.7 114.4 all-gather.6
  504.9 85.1 all-reduce.7
  644.7 85.7 all-reduce.9
  770.0 85.8 all-reduce.11
  1365.4 110.7 reduce-scatter.11
  1478.5 111.2 reduce-scatter.13
  1593.4 64.2 reduce-scatter.21
  1661.2 60.2 reduce-scatter.23
  1725.6 59.0 reduce-scatter.15
  1789.1 74.6 reduce-scatter.19
  1868.1 74.7 reduce-scatter.17
Sparse Core Ops, SparseCore 1:
  507.5 41.7 all-gather.10
  551.4 40.9 all-gather.12
  1617.9 120.2 all-reduce.15
  1740.4 85.7 all-reduce.13
